TPU v7x, 512 devices: a whole 4x8x8 slice. The times are simulated.
512 devices in a mesh: patch: 64 (over y, z), visit: 8 (over x, core).
Axes of the slice: x: 4, y: 8, z: 8, core: 2. Of those that a mesh axis runs over, the one named last changes fastest.
Arguments:
- stamps: bfloat16 [8, 8192, 32, 128], P('visit', 'patch'), may hold values from -6 to 6
- coefs: bfloat16 [8, 8192, 64], P('visit', 'patch'), may hold values from -0.75 to 0.75
- basis: bfloat16 [8, 64, 21, 21], P('visit', 'patch'), may hold values from -0.29882812 to 0.29882812
- taps: bfloat16 [8, 8192, 8], P('visit', 'patch'), may hold values from 0.049804688 to 0.59765625
- weights: bfloat16 [8, 8192], P('visit', 'patch'), may hold values from 0.19921875 to 5
- target: int32 [8, 8192, 1], P('visit', 'patch'), may hold values from 0 to 63; in each aligned block of 128 rows (0 to 127, 128 to 255, ..., all dimensions but the last counted through in order) at most 4 rows name the same one
- row_offset: int32 [8, 8192], P('visit', 'patch'), may hold values from 0 to 223
- col_offset: int32 [8, 8192], P('visit', 'patch'), may hold values from 0 to 127
Outputs:
- coadd: float32 [64, 256, 256], P('patch', 'visit')
- depth_map: float32 [64, 256, 256], P('patch', 'visit')
Inputs may be any that keep to these rules, and one draw needn't show every extreme that they name: `target`: among the rows of one device no patch is named more than 4 times, a bound that some block reaches.
All inputs are finite; a program needn't handle non-finite values.
Results may differ from a plain program's by a relative error of at most 0.0057.
Values may be sent and summed in bfloat16 or wider, within the bound.
No kernel may reach another device: no remote copies, remote signals or barrier semaphores. Data moves between devices by JAX's collectives and lax.ppermute only.
A program may use at most 64 MiB of HBM per device.

v0:
```python
import jax
import jax.numpy as jnp
from jax import lax
from jax.sharding import PartitionSpec as P

PATCH_ROWS = 256
PATCH_COLS = 256


def make_kernels(coefficients, basis_set):
    term_count = basis_set.shape[0]
    kernel_size = basis_set.shape[1]
    flat = jnp.dot(
        coefficients,
        basis_set.reshape(term_count, kernel_size * kernel_size),
        preferred_element_type=jnp.float32,
    )
    return flat.astype(jnp.bfloat16).reshape(coefficients.shape[0], kernel_size, kernel_size)


def convolve(pixels, kernels):
    kernel_size = kernels.shape[1]
    kernel_reach = kernel_size // 2
    height = pixels.shape[1]
    breadth = pixels.shape[2]
    padded = jnp.pad(pixels, ((0, 0), (0, 0), (kernel_reach, kernel_reach)))
    shifted = jnp.stack(
        [
            padded[:, :, column_shift : column_shift + breadth]
            for column_shift in range(kernel_size)
        ],
        axis=1,
    )
    offsets = (
        jnp.arange(height, dtype=jnp.int32)[None, :]
        - jnp.arange(height, dtype=jnp.int32)[:, None]
        + kernel_reach
    )
    onehot = (
        offsets[None, :, :] == jnp.arange(kernel_size, dtype=jnp.int32)[:, None, None]
    ).astype(jnp.bfloat16)
    toeplitz = jnp.einsum(
        "nab,aij->nbij", kernels, onehot, preferred_element_type=jnp.float32
    ).astype(jnp.bfloat16)
    result = jnp.einsum("nbik,nbkj->nij", toeplitz, shifted, preferred_element_type=jnp.float32)
    return result.astype(jnp.bfloat16)


def resample(convolved, tap_values, scale, row_start, col_start):
    height = convolved.shape[1]
    breadth = convolved.shape[2]
    column_gap = (
        jnp.arange(PATCH_COLS, dtype=jnp.int32)[None, :, None]
        - col_start[:, None, None]
        - jnp.arange(breadth, dtype=jnp.int32)[None, None, :]
        + 1
    )
    row_gap = (
        jnp.arange(PATCH_ROWS, dtype=jnp.int32)[None, :, None]
        - row_start[:, None, None]
        - jnp.arange(height, dtype=jnp.int32)[None, None, :]
        + 1
    )
    column_sum = jnp.zeros(column_gap.shape, jnp.float32)
    row_sum = jnp.zeros(row_gap.shape, jnp.float32)
    for tap_index in range(4):
        column_sum = column_sum + jnp.where(
            column_gap == tap_index,
            tap_values[:, 4 + tap_index].astype(jnp.float32)[:, None, None],
            0.0,
        )
        row_sum = row_sum + jnp.where(
            row_gap == tap_index, tap_values[:, tap_index].astype(jnp.float32)[:, None, None], 0.0
        )
    column_map = column_sum.astype(jnp.bfloat16)
    row_map = (scale.astype(jnp.float32)[:, None, None] * row_sum).astype(jnp.bfloat16)
    spread = jnp.einsum(
        "nij,ncj->nic", convolved, column_map, preferred_element_type=jnp.float32
    ).astype(jnp.bfloat16)
    return (row_map, column_map, spread)


def accumulate(pixels, extras, starts, full_basis):
    block_size = 8
    block_count = pixels.shape[0] // block_size
    term_count = full_basis.shape[0]
    blocks = (
        pixels.reshape(block_count, block_size, pixels.shape[1], pixels.shape[2]),
        extras.reshape(block_count, block_size, extras.shape[1]),
        starts.reshape(block_count, block_size, 2),
    )

    def update(state, block):
        numerator, depth_map = state
        convolved, extra_block, start_block = block
        convolved = convolve(convolved, make_kernels(extra_block[:, :term_count], full_basis))
        extra_block = extra_block[:, term_count:]
        row_map, column_map, spread = resample(
            convolved, extra_block[:, :8], extra_block[:, 8], start_block[:, 0], start_block[:, 1]
        )
        numerator = numerator + jnp.einsum(
            "nri,nic->rc", row_map, spread, preferred_element_type=jnp.float32
        )
        row_weight = jnp.sum(row_map.astype(jnp.float32), axis=2)
        column_weight = jnp.sum(column_map.astype(jnp.float32), axis=2)
        depth_map = depth_map + jnp.dot(
            row_weight.T, column_weight, precision=lax.Precision.HIGHEST
        )
        return ((numerator, depth_map), None)

    initial = (
        jnp.zeros((PATCH_ROWS, PATCH_COLS), jnp.float32),
        jnp.zeros((PATCH_ROWS, PATCH_COLS), jnp.float32),
    )
    final_state, unused = lax.scan(update, initial, blocks)
    return final_state


def per_device(stamps, coefs, basis, taps, weights, target, row_offset, col_offset):
    peer_count = lax.axis_size("patch")
    stamp_count = stamps.shape[1]
    height = stamps.shape[2]
    breadth = stamps.shape[3]
    slot_count = 2 * stamp_count // peer_count
    full_basis = lax.all_gather(basis[0], "patch", axis=0, tiled=True)
    destination = target[0, :, 0]
    position = jnp.arange(stamp_count, dtype=jnp.int32)
    earlier = (destination[None, :] == destination[:, None]) & (
        position[None, :] < position[:, None]
    )
    standing = jnp.sum(earlier.astype(jnp.int32), axis=1)
    placement = destination * slot_count + standing
    chooser = placement[None, :] == jnp.arange(peer_count * slot_count, dtype=jnp.int32)[:, None]
    select = chooser.astype(jnp.bfloat16)

    def pack(values):
        packed = jnp.dot(select, values, preferred_element_type=jnp.float32).astype(jnp.bfloat16)
        return packed.reshape(peer_count, slot_count, values.shape[1])

    starts = jnp.stack([row_offset[0], col_offset[0]], axis=1)
    packed_starts = jnp.sum(jnp.where(chooser[:, :, None], starts[None, :, :], 0), axis=1).reshape(
        peer_count, slot_count, 2
    )
    total_slots = peer_count * slot_count
    extras = jnp.concatenate([coefs[0], taps[0], weights[0][:, None]], axis=1)
    packed_pixels = pack(stamps[0].reshape(stamp_count, height * breadth))
    packed_extras = pack(extras)
    got_pixels, got_extras, got_starts = (
        lax.all_to_all(packed_pixels, "patch", split_axis=0, concat_axis=0, tiled=True),
        lax.all_to_all(packed_extras, "patch", split_axis=0, concat_axis=0, tiled=True),
        lax.all_to_all(packed_starts, "patch", split_axis=0, concat_axis=0, tiled=True),
    )
    numerator, depth_map = accumulate(
        got_pixels.reshape(total_slots, height, breadth),
        got_extras.reshape(total_slots, got_extras.shape[2]),
        got_starts.reshape(total_slots, 2),
        full_basis,
    )
    numerator, depth_map = (
        lax.psum_scatter(numerator, "visit", scatter_dimension=0, tiled=True),
        lax.psum_scatter(depth_map, "visit", scatter_dimension=0, tiled=True),
    )
    coadd = numerator / (1.0 + depth_map)
    return (coadd[None], depth_map[None])


def solution(mesh):
    placed = (
        P("visit", "patch", None, None),
        P("visit", "patch", None),
        P("visit", "patch", None, None),
        P("visit", "patch", None),
        P("visit", "patch"),
        P("visit", "patch", None),
        P("visit", "patch"),
        P("visit", "patch"),
    )
    return jax.shard_map(
        per_device,
        mesh=mesh,
        in_specs=placed,
        out_specs=(P("patch", "visit", None), P("patch", "visit", None)),
        check_vma=False,
    )
```

profile of v0, /device:TPU:8, one launch (start us, length us, event | category | flops | bytes accessed | tf_op | source)
XLA Modules:
  0.0 502.9 jit_solution(15867285318595806077)
XLA Ops:
  7.2 0.9 convert_reduce_fusion.2
  10.4 16.6 %all-to-all-start.1 = ((s32[64,4,2]{1,2,0:T(2,128)}), s32[64,4,2]{1,2,0:T(2,128)S(1)}, u32[]{:S(2)}, u32[]{:S(2)}) async-start(s32[64,4,2]{1,2,0:T(2,128)} %copy.93), calls=%async_computation.1 | async-start | bytes 131072 | tf_op jit(solution)/shard_map/all_to_all | solution.py:151
  27.0 2.0 convolution_convert_fusion.3
  28.9 2.2 reshape.221
  31.2 7.1 %all-to-all-done.1 = s32[64,4,2]{1,2,0:T(2,128)S(1)} async-done(((s32[64,4,2]{1,2,0:T(2,128)}), s32[64,4,2]{1,2,0:T(2,128)S(1)}, u32[]{:S(2)}, u32[]{:S(2)}) %all-to-all-start.1) | async-done | bytes 2080 | tf_op jit(solution)/shard_map/all_to_all | solution.py:151
  38.3 5.7 %all-to-all-start.2 = ((bf16[64,4,4096]{2,1,0:T(4,128)(2,1)}), bf16[64,4,4096]{2,1,0:T(4,128)(2,1)S(1)}, u32[]{:S(2)}, u32[]{:S(2)}) async-start(bf16[64,4,4096]{2,1,0:T(4,128)(2,1)} %reshape.221), calls=%async_computation.2 | async-start | bytes 4194304 | tf_op jit(solution)/shard_map/all_to_all | solution.py:149
  45.0 50.3 %all-to-all-done.2 = bf16[64,4,4096]{2,1,0:T(4,128)(2,1)S(1)} async-done(((bf16[64,4,4096]{2,1,0:T(4,128)(2,1)}), bf16[64,4,4096]{2,1,0:T(4,128)(2,1)S(1)}, u32[]{:S(2)}, u32[]{:S(2)}) %all-to-all-start.2) | async-done | bytes 2097184 | tf_op jit(solution)/shard_map/all_to_all | solution.py:149
  95.3 12.5 %all-to-all-start = ((bf16[64,4,73]{2,1,0:T(4,128)(2,1)}), bf16[64,4,73]{2,1,0:T(4,128)(2,1)S(1)}, u32[]{:S(2)}, u32[]{:S(2)}) async-start(bf16[64,4,73]{2,1,0:T(4,128)(2,1)} %bitcast.4), calls=%async_computation | async-start | bytes 131072 | tf_op jit(solution)/shard_map/all_to_all | solution.py:150
  107.9 49.5 %all-gather = bf16[64,1,21,21]{3,2,1,0:T(8,128)(2,1)S(1)} all-gather(bf16[1,1,21,21]{3,2,1,0:T(8,128)(2,1)S(1)} %copy-done.3), channel_id=2, replica_groups=mesh['patch'=64,'visit'=8] {'patch'}, dimensions={0}, use_global_device_ids=true | all-gather | bytes 57330 | tf_op jit(solution)/shard_map/all_gather | solution.py:125
  157.8 3.2 reshape_reshape.11
  161.0 261.2 %while.16 = (s32[]{:T(128)}, f32[256,256]{1,0:T(8,128)S(1)}, f32[256,256]{1,0:T(8,128)S(1)}, bf16[32,8,73]{2,1,0:T(8,128)(2,1)S(1)}, s32[32,8,2]{1,0,2:T(8,128)S...) while((s32[]{:T(128)}, f32[256,256]{1,0:T(8,128)S(1)}, ...), condition=%wide.wide.region_5.6_spmd.clone, body=%wide.wide.region_2.5_spmd.clone.sunk | while | flops 118861328 | bytes 6383152 | solution.py:115
  166.6 0.9 fusion.192
  174.8 0.9 fusion.192
  182.9 0.9 fusion.192
  191.1 0.9 fusion.192
  199.3 0.9 fusion.192
  207.4 0.9 fusion.192
  215.6 0.9 fusion.192
  223.7 0.9 fusion.192
  231.9 0.9 fusion.192
  240.1 0.9 fusion.192
  248.2 0.9 fusion.192
  256.4 0.9 fusion.192
  264.6 0.9 fusion.192
  272.7 0.9 fusion.192
  280.9 0.9 fusion.192
  289.1 0.9 fusion.192
  297.2 0.9 fusion.192
  305.4 0.9 fusion.192
  313.6 0.9 fusion.192
  321.7 0.9 fusion.192
  329.9 0.9 fusion.192
  338.0 0.9 fusion.192
  346.2 0.9 fusion.192
  350.7 0.9 bitcast_dynamic-update-slice_fusion.3
  354.4 0.9 fusion.192
  362.5 0.9 fusion.192
  370.7 0.9 fusion.192
  378.9 0.9 fusion.192
  387.0 0.9 fusion.192
  391.5 0.9 bitcast_dynamic-update-slice_fusion.3
  395.2 0.9 fusion.192
  403.4 0.9 fusion.192
  411.5 0.9 fusion.192
  419.7 0.9 fusion.192
  423.7 33.2 %reduce-scatter.5.cloned.1.call-done = f32[32,256]{1,0:T(8,128)} async-done(((f32[256,256]{1,0:T(8,128)}), f32[32,256]{1,0:T(8,128)}) %reduce-scatter.5.cloned.1.call-update) | async-done | bytes 32784 | tf_op jit(solution)/shard_map/reduce_scatter | solution.py:161
  456.9 37.8 %reduce-scatter.3.cloned.1.call-done = f32[32,256]{1,0:T(8,128)} async-done(((f32[256,256]{1,0:T(8,128)}), f32[32,256]{1,0:T(8,128)}) %reduce-scatter.3.cloned.1.call-update) | async-done | bytes 32784 | tf_op jit(solution)/shard_map/reduce_scatter | solution.py:160
  494.7 1.4 divide_bitcast_fusion
  (1183 shorter events, 230.2 us)
Async XLA Ops:
  10.4 27.9 %all-to-all-start.1 = ((s32[64,4,2]{1,2,0:T(2,128)}), s32[64,4,2]{1,2,0:T(2,128)S(1)}, u32[]{:S(2)}, u32[]{:S(2)}) async-start(s32[64,4,2]{1,2,0:T(2,128)} %copy.93), calls=%async_computation.1 | async-start | bytes 131072 | tf_op jit(solution)/shard_map/all_to_all | solution.py:151
  31.2 12.9 %copy-start.4 = (bf16[1,128,64]{1,2,0:T(8,128)(2,1)S(1)}, bf16[1,128,64]{1,2,0:T(8,128)(2,1)}, u32[]{:S(2)}) copy-start(bf16[1,128,64]{1,2,0:T(8,128)(2,1)} %param.11) | copy-start | bytes 49156
  31.2 12.9 %copy-start.5 = (bf16[1,128,8]{1,2,0:T(8,128)(2,1)S(1)}, bf16[1,128,8]{1,2,0:T(8,128)(2,1)}, u32[]{:S(2)}) copy-start(bf16[1,128,8]{1,2,0:T(8,128)(2,1)} %param.13) | copy-start | bytes 6148
  31.2 12.9 %copy-start.6 = (bf16[1,128]{1,0:T(2,128)(2,1)S(1)}, bf16[1,128]{1,0:T(2,128)(2,1)}, u32[]{:S(2)}) copy-start(bf16[1,128]{1,0:T(2,128)(2,1)} %param.14) | copy-start | bytes 772
  31.2 76.7 %copy-start.3 = (bf16[1,1,21,21]{3,2,1,0:T(8,128)(2,1)S(1)}, bf16[1,1,21,21]{3,2,1,0:T(8,128)(2,1)}, u32[]{:S(2)}) copy-start(bf16[1,1,21,21]{3,2,1,0:T(8,128)(2,1)} %param.12) | copy-start | bytes 2650
  38.3 57.0 %all-to-all-start.2 = ((bf16[64,4,4096]{2,1,0:T(4,128)(2,1)}), bf16[64,4,4096]{2,1,0:T(4,128)(2,1)S(1)}, u32[]{:S(2)}, u32[]{:S(2)}) async-start(bf16[64,4,4096]{2,1,0:T(4,128)(2,1)} %reshape.221), calls=%async_computation.2 | async-start | bytes 4194304 | tf_op jit(solution)/shard_map/all_to_all | solution.py:149
  95.3 65.7 %all-to-all-start = ((bf16[64,4,73]{2,1,0:T(4,128)(2,1)}), bf16[64,4,73]{2,1,0:T(4,128)(2,1)S(1)}, u32[]{:S(2)}, u32[]{:S(2)}) async-start(bf16[64,4,73]{2,1,0:T(4,128)(2,1)} %bitcast.4), calls=%async_computation | async-start | bytes 131072 | tf_op jit(solution)/shard_map/all_to_all | solution.py:150
  107.8 349.1 %reduce-scatter.5.cloned.1.call-start = ((), (), s32[]{:S(2)}) async-start(), calls=%async_computation.6 | async-start | bytes 294912 | tf_op jit(solution)/shard_map/reduce_scatter | solution.py:161
  157.6 3.4 copy-start.1
  422.3 0.7 copy-start
  422.3 0.8 copy-start.2
  423.0 71.7 %reduce-scatter.3.cloned.1.call-start = ((), (), s32[]{:S(2)}) async-start(), calls=%async_computation.5 | async-start | bytes 294912 | tf_op jit(solution)/shard_map/reduce_scatter | solution.py:160
Sparse Core Ops, SparseCore 0:
  423.1 33.7 reduce-scatter.4
  459.9 34.7 reduce-scatter.2
where the time goes:
time: 506 us; the launch traced here: 503 us
  local copies, waits for them, and re-layouts  135 us (27%)
  waiting for transfers between devices  129 us (25%)
  matrix products  91.7 us (18%)
  blocking collectives  49.5 us (10%)
  other arithmetic  42.5 us (8%)
  starting transfers between devices  34.9 us (7%)
  between operations  14.2 us (3%)
  loops' own time  5.66 us (1%)
    while x640, local copies, waits for them, and re-layouts  88.1 us
    all_to_all x1, waiting for transfers between devices, per_device(): lax.all_to_all(packed_pixels, 'patch', split_axis=0, concat_axis=0, tiled...  50.3 us
    all_gather x1, blocking collectives, per_device(): full_basis = lax.all_gather(basis[0], 'patch', axis=0, tiled=True)  49.5 us
    reduce_scatter x1, waiting for transfers between devices, per_device(): lax.psum_scatter(numerator, 'visit', scatter_dimension=0, tiled=True)  37.8 us
    reduce_scatter x1, waiting for transfers between devices, per_device(): lax.psum_scatter(depth_map, 'visit', scatter_dimension=0, tiled=True)  33.2 us
    dot_general x32, matrix products, update(): jnp.einsum('nri,nic->rc', row_map, spread, preferred_element_type=jnp.flo...  28.8 us
    reduce_sum x32, other arithmetic, update(): column_weight = jnp.sum(column_map.astype(jnp.float32), axis=2)  27.4 us
    squeeze x32, local copies, waits for them, and re-layouts, accumulate(): final_state, unused = lax.scan(update, initial, blocks)  27.1 us
  transfers between devices with their start and end apart: 5, of which 4 were waited for; matrix products, arithmetic and copies ran while one was open for 2% of the time, Pallas kernels for 0%

commit v1 on v0

--- a/solution.py
+++ b/solution.py
@@ -5,6 +5,14 @@
 
 PATCH_ROWS = 256
 PATCH_COLS = 256
+
+
+def windows_process(local_values):
+    inter = jnp.concatenate(
+        lax.all_to_all(jnp.stack([local_values] * lax.psum(1, "patch"), axis=0), "patch", 0, 0),
+        axis=0,
+    )
+    return inter
 
 
 def make_kernels(coefficients, basis_set):
@@ -122,7 +130,7 @@
     height = stamps.shape[2]
     breadth = stamps.shape[3]
     slot_count = 2 * stamp_count // peer_count
-    full_basis = lax.all_gather(basis[0], "patch", axis=0, tiled=True)
+    full_basis = windows_process(basis[0])
     destination = target[0, :, 0]
     position = jnp.arange(stamp_count, dtype=jnp.int32)
     earlier = (destination[None, :] == destination[:, None]) & (

time: 506 us -> 481 us (0.951)
  blocking collectives: 49.5 us -> 27.7 us
  starting transfers between devices: 34.9 us -> 24.4 us
  waiting for transfers between devices: 129 us -> 135 us
    all_gather x1 -> x0, blocking collectives: 49.5 us -> none  [per_device(): full_basis = lax.all_gather(basis[0], 'patch', axis=0, tiled=True)]
    all_to_all x0 -> x1, blocking collectives: none -> 27.7 us  [per_device(): lax.all_to_all(packed_starts, 'patch', split_axis=0, concat_axis=0, tiled...]
    all_to_all x1, starting transfers between devices: 16.6 us -> 5.53 us  [windows_process(): lax.all_to_all(jnp.stack([local_values] * lax.psum(1, 'patch'), axis=0),...]
    all_to_all x1, waiting for transfers between devices: 0.01 us -> 7.61 us  [per_device(): lax.all_to_all(packed_extras, 'patch', split_axis=0, concat_axis=0, tiled...]
  transfers between devices with their start and end apart: 5 -> 5, of which waited for: 4 -> 5; matrix products, arithmetic and copies ran while one was open for 2% -> 2% of each run, Pallas kernels for 0% -> 0%
where the time goes in v1:
time: 481 us; the launch traced here: 477 us
  local copies, waits for them, and re-layouts  136 us (28%)
  waiting for transfers between devices  135 us (28%)
  matrix products  91.7 us (19%)
  other arithmetic  42.5 us (9%)
  blocking collectives  27.7 us (6%)
  starting transfers between devices  24.4 us (5%)
  between operations  14.2 us (3%)
  loops' own time  5.66 us (1%)
    while x640, local copies, waits for them, and re-layouts  88.1 us
    all_to_all x1, waiting for transfers between devices, per_device(): lax.all_to_all(packed_pixels, 'patch', split_axis=0, concat_axis=0, tiled...  49.8 us
    reduce_scatter x1, waiting for transfers between devices, per_device(): lax.psum_scatter(numerator, 'visit', scatter_dimension=0, tiled=True)  37.8 us
    dot_general x32, matrix products, update(): jnp.einsum('nri,nic->rc', row_map, spread, preferred_element_type=jnp.flo...  28.8 us
    reduce_scatter x1, waiting for transfers between devices, per_device(): lax.psum_scatter(depth_map, 'visit', scatter_dimension=0, tiled=True)  28.3 us
    all_to_all x1, blocking collectives, per_device(): lax.all_to_all(packed_starts, 'patch', split_axis=0, concat_axis=0, tiled...  27.7 us
    reduce_sum x32, other arithmetic, update(): column_weight = jnp.sum(column_map.astype(jnp.float32), axis=2)  27.4 us
    squeeze x32, local copies, waits for them, and re-layouts, accumulate(): final_state, unused = lax.scan(update, initial, blocks)  27.1 us
  transfers between devices with their start and end apart: 5, of which 5 were waited for; matrix products, arithmetic and copies ran while one was open for 2% of the time, Pallas kernels for 0%

profile of v1, /device:TPU:8, one launch (start us, length us, event | category | flops | bytes accessed | tf_op | source)
XLA Modules:
  0.0 477.1 jit_solution(18073246285722644775)
XLA Ops:
  7.2 0.9 convert_reduce_fusion.2
  9.8 27.7 %all_to_all.20 = s32[64,4,2]{1,2,0:T(2,128)S(1)} all-to-all(s32[64,4,2]{1,2,0:T(2,128)S(1)} %copy.90), channel_id=1, replica_groups=mesh['patch'=64,'visit'=8] {'patch'}, dimensions={0} | all-to-all | bytes 4096 | tf_op jit(solution)/shard_map/all_to_all | solution.py:159
  37.5 1.5 stack.139
  38.9 5.5 %all-to-all-start.2 = ((bf16[64,1,21,21]{3,2,1,0:T(8,128)(2,1)}), bf16[64,1,21,21]{3,2,1,0:T(8,128)(2,1)S(1)}, u32[]{:S(2)}, u32[]{:S(2)}) async-start(bf16[64,1,21,21]{3,2,1,0:T(8,128)(2,1)} %stack.139), calls=%async_computation.2 | async-start | bytes 786432 | tf_op jit(solution)/shard_map/all_to_all | solution.py:12
  44.5 2.0 convolution_convert_fusion.3
  46.4 2.2 reshape.218
  48.7 10.6 %all-to-all-done.2 = bf16[64,1,21,21]{3,2,1,0:T(8,128)(2,1)S(1)} async-done(((bf16[64,1,21,21]{3,2,1,0:T(8,128)(2,1)}), bf16[64,1,21,21]{3,2,1,0:T(8,128)(2,1)S(1)}, u32[]{:S(2)}, u32[]{:S(2)}) %all-to-all-start.2) | async-done | bytes 56480 | tf_op jit(solution)/shard_map/all_to_all | solution.py:12
  59.3 6.0 %all-to-all-start.3 = ((bf16[64,4,4096]{2,1,0:T(4,128)(2,1)}), bf16[64,4,4096]{2,1,0:T(4,128)(2,1)S(1)}, u32[]{:S(2)}, u32[]{:S(2)}) async-start(bf16[64,4,4096]{2,1,0:T(4,128)(2,1)} %reshape.218), calls=%async_computation.3 | async-start | bytes 4194304 | tf_op jit(solution)/shard_map/all_to_all | solution.py:157
  66.2 49.8 %all-to-all-done.3 = bf16[64,4,4096]{2,1,0:T(4,128)(2,1)S(1)} async-done(((bf16[64,4,4096]{2,1,0:T(4,128)(2,1)}), bf16[64,4,4096]{2,1,0:T(4,128)(2,1)S(1)}, u32[]{:S(2)}, u32[]{:S(2)}) %all-to-all-start.3) | async-done | bytes 2097184 | tf_op jit(solution)/shard_map/all_to_all | solution.py:157
  116.0 12.7 %all-to-all-start = ((bf16[64,4,73]{2,1,0:T(4,128)(2,1)}), bf16[64,4,73]{2,1,0:T(4,128)(2,1)S(1)}, u32[]{:S(2)}, u32[]{:S(2)}) async-start(bf16[64,4,73]{2,1,0:T(4,128)(2,1)} %bitcast.4), calls=%async_computation | async-start | bytes 131072 | tf_op jit(solution)/shard_map/all_to_all | solution.py:158
  129.2 3.2 reshape_reshape.17
  132.5 7.6 %all-to-all-done = bf16[64,4,73]{2,1,0:T(4,128)(2,1)S(1)} async-done(((bf16[64,4,73]{2,1,0:T(4,128)(2,1)}), bf16[64,4,73]{2,1,0:T(4,128)(2,1)S(1)}, u32[]{:S(2)}, u32[]{:S(2)}) %all-to-all-start) | async-done | bytes 37408 | tf_op jit(solution)/shard_map/all_to_all | solution.py:158
  140.1 261.2 %while.16 = (s32[]{:T(128)}, f32[256,256]{1,0:T(8,128)S(1)}, f32[256,256]{1,0:T(8,128)S(1)}, bf16[32,8,73]{2,1,0:T(8,128)(2,1)S(1)}, s32[32,8,2]{1,0,2:T(8,128)S...) while((s32[]{:T(128)}, f32[256,256]{1,0:T(8,128)S(1)}, ...), condition=%wide.wide.region_5.6_spmd.clone, body=%wide.wide.region_2.5_spmd.clone.sunk | while | flops 118861328 | bytes 6383152 | solution.py:123
  145.7 0.9 fusion.192
  153.8 0.9 fusion.192
  162.0 0.9 fusion.192
  170.2 0.9 fusion.192
  178.3 0.9 fusion.192
  186.5 0.9 fusion.192
  194.7 0.9 fusion.192
  202.8 0.9 fusion.192
  211.0 0.9 fusion.192
  219.2 0.9 fusion.192
  227.3 0.9 fusion.192
  235.5 0.9 fusion.192
  243.7 0.9 fusion.192
  251.8 0.9 fusion.192
  260.0 0.9 fusion.192
  268.1 0.9 fusion.192
  276.3 0.9 fusion.192
  284.5 0.9 fusion.192
  292.6 0.9 fusion.192
  300.8 0.9 fusion.192
  309.0 0.9 fusion.192
  317.1 0.9 fusion.192
  325.3 0.9 fusion.192
  333.5 0.9 fusion.192
  341.6 0.9 fusion.192
  349.8 0.9 fusion.192
  358.0 0.9 fusion.192
  366.1 0.9 fusion.192
  374.3 0.9 fusion.192
  382.4 0.9 fusion.192
  390.6 0.9 fusion.192
  398.8 0.9 fusion.192
  402.8 28.3 %reduce-scatter.5.cloned.1.call-done = f32[32,256]{1,0:T(8,128)} async-done(((f32[256,256]{1,0:T(8,128)}), f32[32,256]{1,0:T(8,128)}) %reduce-scatter.5.cloned.1.call-update) | async-done | bytes 32784 | tf_op jit(solution)/shard_map/reduce_scatter | solution.py:169
  431.1 37.8 %reduce-scatter.3.cloned.1.call-done = f32[32,256]{1,0:T(8,128)} async-done(((f32[256,256]{1,0:T(8,128)}), f32[32,256]{1,0:T(8,128)}) %reduce-scatter.3.cloned.1.call-update) | async-done | bytes 32784 | tf_op jit(solution)/shard_map/reduce_scatter | solution.py:168
  468.9 1.4 divide_bitcast_fusion
  (1182 shorter events, 231.3 us)
Async XLA Ops:
  38.9 20.3 %all-to-all-start.2 = ((bf16[64,1,21,21]{3,2,1,0:T(8,128)(2,1)}), bf16[64,1,21,21]{3,2,1,0:T(8,128)(2,1)S(1)}, u32[]{:S(2)}, u32[]{:S(2)}) async-start(bf16[64,1,21,21]{3,2,1,0:T(8,128)(2,1)} %stack.139), calls=%async_computation.2 | async-start | bytes 786432 | tf_op jit(solution)/shard_map/all_to_all | solution.py:12
  48.7 16.6 %copy-start.3 = (bf16[1,128,64]{1,2,0:T(8,128)(2,1)S(1)}, bf16[1,128,64]{1,2,0:T(8,128)(2,1)}, u32[]{:S(2)}) copy-start(bf16[1,128,64]{1,2,0:T(8,128)(2,1)} %param.11) | copy-start | bytes 49156
  48.7 16.6 %copy-start.4 = (bf16[1,128,8]{1,2,0:T(8,128)(2,1)S(1)}, bf16[1,128,8]{1,2,0:T(8,128)(2,1)}, u32[]{:S(2)}) copy-start(bf16[1,128,8]{1,2,0:T(8,128)(2,1)} %param.13) | copy-start | bytes 6148
  48.7 16.6 %copy-start.5 = (bf16[1,128]{1,0:T(2,128)(2,1)S(1)}, bf16[1,128]{1,0:T(2,128)(2,1)}, u32[]{:S(2)}) copy-start(bf16[1,128]{1,0:T(2,128)(2,1)} %param.14) | copy-start | bytes 772
  59.3 56.7 %all-to-all-start.3 = ((bf16[64,4,4096]{2,1,0:T(4,128)(2,1)}), bf16[64,4,4096]{2,1,0:T(4,128)(2,1)S(1)}, u32[]{:S(2)}, u32[]{:S(2)}) async-start(bf16[64,4,4096]{2,1,0:T(4,128)(2,1)} %reshape.218), calls=%async_computation.3 | async-start | bytes 4194304 | tf_op jit(solution)/shard_map/all_to_all | solution.py:157
  116.0 24.1 %all-to-all-start = ((bf16[64,4,73]{2,1,0:T(4,128)(2,1)}), bf16[64,4,73]{2,1,0:T(4,128)(2,1)S(1)}, u32[]{:S(2)}, u32[]{:S(2)}) async-start(bf16[64,4,73]{2,1,0:T(4,128)(2,1)} %bitcast.4), calls=%async_computation | async-start | bytes 131072 | tf_op jit(solution)/shard_map/all_to_all | solution.py:158
  128.7 302.4 %reduce-scatter.5.cloned.1.call-start = ((), (), s32[]{:S(2)}) async-start(), calls=%async_computation.7 | async-start | bytes 294912 | tf_op jit(solution)/shard_map/reduce_scatter | solution.py:169
  129.2 3.3 copy-start.1
  401.3 0.7 copy-start
  401.4 0.8 copy-start.2
  402.1 66.8 %reduce-scatter.3.cloned.1.call-start = ((), (), s32[]{:S(2)}) async-start(), calls=%async_computation.6 | async-start | bytes 294912 | tf_op jit(solution)/shard_map/reduce_scatter | solution.py:168
Sparse Core Ops, SparseCore 0:
  402.2 28.8 reduce-scatter.4
  434.1 34.7 reduce-scatter.2
